TPU v7x, 32 devices: a whole 2x2x4 slice. The times are simulated.
32 devices in a mesh: gx: 4 (over y, x), gy: 2 (over core), gz: 4 (over z).
Axes of the slice: x: 2, y: 2, z: 4, core: 2. Of those that a mesh axis runs over, the one named last changes fastest.
Arguments:
- frac: float32 [3, 4, 2, 8, 128], P(None, 'gx', 'gy', 'gz'), may hold values from 0 to 1
- velocity: float32 [3, 4, 2, 8, 128], P(None, 'gx', 'gy', 'gz'), may hold values from -2 to 2
- force_old: float32 [3, 4, 2, 8, 128], P(None, 'gx', 'gy', 'gz'), may hold values from -6 to 6
- species: int32 [4, 2, 8, 128], P('gx', 'gy', 'gz'), may hold values from 0 to 9
- cell_count: int32 [4, 2, 8], P('gx', 'gy', 'gz'), may hold values from 1 to 128, as said below
- neighbours: int32 [16, 4, 2, 8, 128], P(None, 'gx', 'gy', 'gz'), may hold values from 0 to 3455, as said below
- embed: bfloat16 [10, 64], replicated, may hold values from -6 to 6
- w_radial_in: bfloat16 [8, 64], replicated, may hold values from -2 to 2
- w_radial_out: bfloat16 [64, 192], replicated, may hold values from -0.75 to 0.75
- w_node: bfloat16 [256, 64], replicated, may hold values from -0.375 to 0.375
- w_energy: float32 [64], replicated, may hold values from -0.75 to 0.75
Outputs:
- next_frac: float32 [3, 4, 2, 8, 128], P(None, 'gx', 'gy', 'gz')
- next_velocity: float32 [3, 4, 2, 8, 128], P(None, 'gx', 'gy', 'gz')
- next_force: float32 [3, 4, 2, 8, 128], P(None, 'gx', 'gy', 'gz')
- site_energy: float32 [4, 2, 8, 128], P('gx', 'gy', 'gz')
Inputs may be any that keep to these rules, and one draw needn't show every extreme that they name: `cell_count`: in every draw at least one cell holds exactly 128 atoms; the other cells hold 1 to 128. `neighbours`: each code o * 128 + s names slot s of the cell at offset (o // 9 - 1, (o // 3) % 3 - 1, o % 3 - 1) from the receiver's cell, periodic; s is below that cell's count; no code names the receiver itself.
All inputs are finite; a program needn't handle non-finite values.
Results may differ from a plain program's by a relative error of at most 0.015.
Values may be sent and summed in bfloat16 or wider, within the bound.
A program may use at most 64 MiB of HBM per device.

v0:
```python
import jax
import jax.numpy as jnp
from jax import lax
from jax.sharding import PartitionSpec as P

MASSES = (1.008, 12.011, 14.007, 15.999, 32.06, 22.99, 35.45, 39.098, 24.305, 40.078)
SQRT3 = 1.7320508075688772
HALF_SQRT3 = 0.8660254037844386
TIME_STEP = 0.5


def padded(array, sides, width):
    for axis, dim in sides:
        size, length = (lax.axis_size(axis), array.shape[dim])
        up = [(i, (i + 1) % size) for i in range(size)]
        down = [(j, i) for i, j in up]
        last = lax.slice_in_dim(array, length - width, length, axis=dim)
        leading = lax.slice_in_dim(array, 0, width, axis=dim)
        before = lax.ppermute(last, axis, up)
        after = lax.ppermute(leading, axis, down)
        array = jnp.concatenate([before, array, after], axis=dim)
    return array


def shifted_2(value, axis, steps):
    count = lax.axis_size(axis)
    pairs = [(source, (source + steps) % count) for source in range(count)]
    return lax.ppermute(value, axis, pairs)


def species_mass(species):
    table = jnp.asarray(MASSES, dtype=jnp.float32) / 16.0
    shape_ones = (1,) * species.ndim
    which = species[None] == jnp.arange(len(MASSES), dtype=jnp.int32).reshape((-1,) + shape_ones)
    return jnp.sum(jnp.where(which, table.reshape((-1,) + shape_ones), 0.0), axis=0)


def embed_species(species_flat, embed):
    kinds = embed.shape[0]
    onehot = (species_flat[None, :] == jnp.arange(kinds, dtype=jnp.int32)[:, None]).astype(
        jnp.bfloat16
    )
    return jnp.dot(embed.T, onehot, preferred_element_type=jnp.float32).astype(jnp.bfloat16)


def site_terms(displace, send_feat, own_feat, w_radial_in, w_radial_out, w_node, w_energy):
    basis_count = w_radial_in.shape[0]
    channels = own_feat.shape[0]
    candidates = displace.shape[1]
    block_size = displace.shape[2]
    squared = jnp.sum(displace * displace, axis=0)
    envelope = jnp.maximum(1.0 - squared, 0.0) ** 3
    centres = jnp.arange(basis_count, dtype=jnp.float32) / (basis_count - 1)
    basis_values = jnp.exp(
        -float((basis_count - 1) ** 2) * (squared[None] - centres[:, None, None]) ** 2
    )
    basis_values = basis_values.astype(jnp.bfloat16).reshape(basis_count, candidates * block_size)
    hidden = jax.nn.silu(
        jnp.dot(w_radial_in.T, basis_values, preferred_element_type=jnp.float32)
    ).astype(jnp.bfloat16)
    radial = jnp.dot(w_radial_out.T, hidden, preferred_element_type=jnp.float32)
    radial = radial.reshape(3, channels, candidates, block_size) * envelope[None, None]
    along_x = displace[0]
    along_y = displace[1]
    along_z = displace[2]
    first_order = jnp.stack([along_x, along_y, along_z])
    second_order = jnp.stack(
        [
            SQRT3 * along_x * along_y,
            SQRT3 * along_y * along_z,
            SQRT3 * along_z * along_x,
            HALF_SQRT3 * (along_x * along_x - along_y * along_y),
            0.5 * (2.0 * along_z * along_z - along_x * along_x - along_y * along_y),
        ]
    )
    carried = radial * send_feat.astype(jnp.float32)[None]
    scalar_part = jnp.sum(carried[0], axis=1)
    vector_part = jnp.sum(carried[1][None] * first_order[:, None], axis=2)
    tensor_part = jnp.sum(carried[2][None] * second_order[:, None], axis=2)
    invariant = jnp.concatenate(
        [
            scalar_part,
            jnp.sum(vector_part * vector_part, axis=0),
            jnp.sum(tensor_part * tensor_part, axis=0),
            own_feat.astype(jnp.float32),
        ],
        axis=0,
    ).astype(jnp.bfloat16)
    activity = jax.nn.silu(jnp.dot(w_node.T, invariant, preferred_element_type=jnp.float32))
    return jnp.sum(w_energy[:, None] * activity, axis=0)


def rim_layers(summed, axis_dim):
    length = summed.shape[axis_dim] - 2
    lower = lax.slice_in_dim(summed, 0, 1, axis=axis_dim)
    upper = lax.slice_in_dim(summed, length + 1, length + 2, axis=axis_dim)
    return (lower, upper)


def add_rims(summed, axis_dim, from_above, from_below):
    length = summed.shape[axis_dim] - 2
    middle = lax.slice_in_dim(summed, 1, length + 1, axis=axis_dim)
    widths_low = [(0, 0)] * summed.ndim
    widths_low[axis_dim] = (0, length - 1)
    widths_high = [(0, 0)] * summed.ndim
    widths_high[axis_dim] = (length - 1, 0)
    return middle + jnp.pad(from_below, widths_low) + jnp.pad(from_above, widths_high)


def shards(
    frac,
    velocity,
    force_old,
    species,
    cell_count,
    neighbours,
    embed,
    w_radial_in,
    w_radial_out,
    w_node,
    w_energy,
):
    cells_x, cells_y, cells_z, capacity = species.shape
    candidates = neighbours.shape[0]
    local_slots = cells_x * cells_y * cells_z * capacity
    wide_y = cells_y + 2
    wide_z = cells_z + 2
    block_size = cells_z * capacity
    occupied_int = (
        lax.broadcasted_iota(jnp.int32, species.shape, 3) < cell_count[..., None]
    ).astype(jnp.int32)
    occupied = occupied_int.astype(jnp.float32)
    atom_mass = species_mass(species)
    half_velocity = velocity + 0.5 * TIME_STEP * force_old / atom_mass
    moved = frac + TIME_STEP * half_velocity
    ghost_moved = padded(moved, (("gx", 1), ("gy", 2), ("gz", 3)), 1)
    own_feats = embed_species(species.reshape(local_slots), embed)
    channels = own_feats.shape[0]
    moved_flat = moved.reshape(3, local_slots)
    ghost_pos_flat = ghost_moved.reshape(3, -1)
    codes = neighbours.reshape(candidates, local_slots)
    occupied_flat = occupied.reshape(local_slots)
    receiver_order = jnp.arange(local_slots, dtype=jnp.int32)
    passes = local_slots // block_size
    cell_id = receiver_order // capacity
    cell_a = (cell_id // (cells_y * cells_z))[None, :]
    cell_b = (cell_id // cells_z % cells_y)[None, :]
    cell_c = (cell_id % cells_z)[None, :]
    offset = codes // capacity
    slot_id = codes % capacity
    shift_a = offset // 9 - 1
    shift_b = offset // 3 % 3 - 1
    shift_c = offset % 3 - 1
    senders_all = (
        ((cell_a + 1 + shift_a) * wide_y + cell_b + 1 + shift_b) * wide_z + cell_c + 1 + shift_c
    ) * capacity + slot_id
    cell_shift = jnp.stack([shift_a, shift_b, shift_c]).astype(jnp.float32)
    displace_all = cell_shift + ghost_pos_flat[:, senders_all] - moved_flat[:, None, :]
    ghost_kinds = padded(species, (("gx", 0), ("gy", 1), ("gz", 2)), 1)
    sender_kinds = ghost_kinds.reshape(-1)[senders_all]

    def sender_features():
        return embed_species(sender_kinds.reshape(-1), embed).reshape(
            channels, candidates, block_size
        )

    def one_block(number, carried):
        send_feat = sender_features()

        def energy_of(shifted):
            return site_terms(
                shifted, send_feat, own_feats, w_radial_in, w_radial_out, w_node, w_energy
            )

        energy, pullback = jax.vjp(energy_of, displace_all)
        gradient = pullback(occupied_flat)[0]
        return (gradient, energy)

    start_state = (
        jnp.zeros((3, candidates, local_slots), jnp.float32),
        jnp.zeros((local_slots,), jnp.float32),
    )
    gradients, energies_ord = lax.fori_loop(0, passes, one_block, start_state)
    own_force_ord = jnp.sum(gradients, axis=1)
    sender_force = jnp.zeros((3, (cells_x + 2) * wide_y * wide_z * capacity), jnp.float32)
    sender_force = sender_force.at[:, senders_all.reshape(-1)].add(-gradients.reshape(3, -1))
    extended = sender_force.reshape(3, cells_x + 2, wide_y, wide_z, capacity)
    lower, upper = rim_layers(extended, 1)
    from_above = shifted_2(lower, "gx", -1)
    from_below = shifted_2(upper, "gx", 1)
    extended = add_rims(extended, 1, from_above, from_below)
    lower, upper = rim_layers(extended, 2)
    from_above = shifted_2(lower, "gy", -1)
    from_below = shifted_2(upper, "gy", 1)
    extended = add_rims(extended, 2, from_above, from_below)
    lower, upper = rim_layers(extended, 3)
    from_above = shifted_2(lower, "gz", -1)
    from_below = shifted_2(upper, "gz", 1)
    folded = add_rims(extended, 3, from_above, from_below)
    total_force = own_force_ord.reshape(3, cells_x, cells_y, cells_z, capacity) + folded
    next_force = occupied * total_force
    next_velocity = occupied * (half_velocity + 0.5 * TIME_STEP * next_force / atom_mass)
    next_frac = occupied * moved
    site_energy = occupied * energies_ord.reshape(cells_x, cells_y, cells_z, capacity)
    return (next_frac, next_velocity, next_force, site_energy)


def solution(mesh):
    in_specs = (
        P(None, "gx", "gy", "gz", None),
        P(None, "gx", "gy", "gz", None),
        P(None, "gx", "gy", "gz", None),
        P("gx", "gy", "gz", None),
        P("gx", "gy", "gz"),
        P(None, "gx", "gy", "gz", None),
        P(),
        P(),
        P(),
        P(),
        P(),
    )
    out_specs = (
        P(None, "gx", "gy", "gz", None),
        P(None, "gx", "gy", "gz", None),
        P(None, "gx", "gy", "gz", None),
        P("gx", "gy", "gz", None),
    )
    return jax.shard_map(shards, mesh=mesh, in_specs=in_specs, out_specs=out_specs, check_vma=False)
```

profile of v0, /device:TPU:0, one launch (start us, length us, event | category | flops | bytes accessed | tf_op | source)
XLA Modules:
  0.0 126.0 jit_solution(390282941705008060)
XLA Ops:
  0.6 0.7 fusion.104
  1.4 0.8 fusion.97
  2.2 1.3 %broadcast_multiply_fusion = (f32[3,1,1,2,128]{4,3,2,1,0:T(2,128)}, f32[3,1,1,2,128]{4,3,2,1,0:T(2,128)S(1)}, f32[3,1,1,2,128]{4,3,2,1,0:T(2,128)S(1)}) fusion(f32[2,128]{1,0:T(2,128)S(1)} %fusion.104, f32[3,1,1,2,128]{4,3,2,1,0:T(2,128)} %param.12, f32[3,1,1,2,128]{4,3,2,1,0:T(2,128)} %param.13, f32[2,128]{1,0:T(2,128)S(1)} %fusion.97, ...), kind=kLoop, calls=%fused_computation.220 | loop fusion | flops 4608 | bytes 20480 | tf_op jit(solution)/shard_map/mul | solution.py:203
  3.5 3.0 %collective-permute-start = (f32[3,1,1,2,128]{4,3,2,1,0:T(2,128)S(1)}, f32[3,1,1,2,128]{4,3,2,1,0:T(2,128)S(1)}, u32[]{:S(2)}, u32[]{:S(2)}) collective-permute-start(f32[3,1,1,2,128]{4,3,2,1,0:T(2,128)S(1)} %get-tuple-element.35), channel_id=1, source_target_pairs={{0,8},{8,16},{16,24},{24,0},{1,9},{9,17},{17,25},{25,1},{2,10},{10... | collective-permute-start | bytes 9224 | tf_op jit(solution)/shard_map/ppermute | solution.py:19
  6.5 1.0 collective-permute-start.1
  7.4 1.1 collective-permute-start.6
  8.5 1.9 %collective-permute-start.7 = (s32[1,1,2,128]{3,2,1,0:T(2,128)}, s32[1,1,2,128]{3,2,1,0:T(2,128)S(1)}, u32[]{:S(2)}, u32[]{:S(2)}) collective-permute-start(s32[1,1,2,128]{3,2,1,0:T(2,128)} %param.15), channel_id=1, source_target_pairs={{8,0},{16,8},{24,16},{0,24},{9,1},{17,9},{25,17},{1,25},{10,2},{18... | collective-permute-start | bytes 3080 | tf_op jit(solution)/shard_map/ppermute | solution.py:20
  10.3 0.7 reshape.947
  11.1 0.7 reshape.945
  12.0 0.6 fusion.63
  12.7 1.5 %fusion.16 = bf16[64,256]{1,0:T(8,128)(2,1)} fusion(bf16[10,64]{1,0:T(8,128)(2,1)} %param.18, s32[256]{0:T(256)} %bitcast.129), kind=kOutput, calls=%fused_computation.36 | convolution fusion | flops 346624 | bytes 35072 | tf_op jit(solution)/shard_map/dot_general | solution.py:43
  14.2 1.8 %compare_select_fusion = s32[4096,1]{0,1:T(1,128)} fusion(s32[4096,1]{0,1:T(1,128)S(1)} %bitcast.125, s32[4096,1]{0,1:T(1,128)S(1)} %bitcast.124, s32[4096,1]{0,1:T(1,128)} %bitcast.119), kind=kLoop, calls=%fused_computation.68 | loop fusion | flops 241664 | bytes 65536 | tf_op jit(solution)/shard_map/select_n | solution.py:186
  15.9 0.7 lt.101
  16.6 0.6 fusion.105
  17.2 0.7 constant_dynamic-update-slice_fusion.1
  18.0 0.5 collective-permute-start.9
  18.5 0.6 iota_multiply_fusion
  19.1 0.2 collective-permute-done.9
  19.3 2.1 %collective-permute-start.10 = (s32[3,3,1,128]{3,2,1,0:T(1,128)S(1)}, s32[3,3,1,128]{3,2,1,0:T(1,128)S(1)}, u32[]{:S(2)}, u32[]{:S(2)}) collective-permute-start(s32[3,3,1,128]{3,2,1,0:T(1,128)S(1)} %get-tuple-element.69), channel_id=1, source_target_pairs={{0,1},{1,2},{2,3},{3,0},{4,5},{5,6},{6,7},{7,4},{8,9},{9,10},{10,1... | collective-permute-start | bytes 13832 | tf_op jit(solution)/shard_map/ppermute | solution.py:19
  21.4 2.1 %collective-permute-start.11 = (s32[3,3,1,128]{3,2,1,0:T(1,128)S(1)}, s32[3,3,1,128]{3,2,1,0:T(1,128)S(1)}, u32[]{:S(2)}, u32[]{:S(2)}) collective-permute-start(s32[3,3,1,128]{3,2,1,0:T(1,128)S(1)} %get-tuple-element.70), channel_id=1, source_target_pairs={{1,0},{2,1},{3,2},{0,3},{5,4},{6,5},{7,6},{4,7},{9,8},{10,9},{11,1... | collective-permute-start | bytes 13832 | tf_op jit(solution)/shard_map/ppermute | solution.py:20
  23.7 0.4 collective-permute-start.3
  24.1 1.0 collective-permute-done.10
  25.1 23.0 %gather_fusion.1 = s32[4096]{0:T(1024)S(1)} fusion(s32[4608]{0:T(1024)S(1)} %reshape.949, s32[4096]{0:T(1024)S(1)} %broadcast_clamp_fusion), kind=kCustom, calls=%fused_computation.1 | custom fusion | bytes 49152 | tf_op jit(solution)/shard_map/gather | solution.py:160
  48.3 1.6 %collective-permute-start.4 = (f32[3,3,3,1,128]{4,3,2,1,0:T(1,128)S(1)}, f32[3,3,3,1,128]{4,3,2,1,0:T(1,128)S(1)}, u32[]{:S(2)}, u32[]{:S(2)}) collective-permute-start(f32[3,3,3,1,128]{4,3,2,1,0:T(1,128)S(1)} %get-tuple-element.62), channel_id=1, source_target_pairs={{0,1},{1,2},{2,3},{3,0},{4,5},{5,6},{6,7},{7,4},{8,9},{9,10},{10,1... | collective-permute-start | bytes 41480 | tf_op jit(solution)/shard_map/ppermute | solution.py:19
  49.8 2.6 %collective-permute-start.5 = (f32[3,3,3,1,128]{4,3,2,1,0:T(1,128)S(1)}, f32[3,3,3,1,128]{4,3,2,1,0:T(1,128)S(1)}, u32[]{:S(2)}, u32[]{:S(2)}) collective-permute-start(f32[3,3,3,1,128]{4,3,2,1,0:T(1,128)S(1)} %get-tuple-element.63), channel_id=1, source_target_pairs={{1,0},{2,1},{3,2},{0,3},{5,4},{6,5},{7,6},{4,7},{9,8},{10,9},{11,1... | collective-permute-start | bytes 41480 | tf_op jit(solution)/shard_map/ppermute | solution.py:20
  52.4 0.3 fusion.2
  52.7 0.3 copy.64
  53.1 0.9 collective-permute-done.4
  54.0 0.7 copy.46
  54.7 14.2 %gather_fusion = f32[4096,3]{1,0:T(8,128)} fusion(f32[3,4608]{0,1:T(8,128)S(1)} %bitcast.112, s32[4096]{0:T(1024)S(1)} %broadcast_clamp_fusion), kind=kCustom, calls=%fused_computation | custom fusion | bytes 114688 | tf_op jit(solution)/shard_map/gather | solution.py:158
  68.9 2.2 %copy.47 = f32[16,256,3]{1,0,2:T(8,128)S(1)} copy(f32[16,256,3]{2,1,0:T(8,128)} %bitcast.114) | data formatting | bytes 98304 | tf_op jit(solution)/shard_map/gather | solution.py:158
  71.1 0.7 multiply_reduce_fusion.9
  71.9 1.0 convolution_bitcast_fusion
  72.9 0.6 fusion.22
  73.6 0.3 copy-done.1
  73.9 1.2 copy.62
  75.1 0.6 fusion.8
  75.7 0.4 slice_reduce_fusion
  76.2 0.8 multiply_reduce_fusion.5
  77.0 1.4 %multiply_reduce_fusion.2 = f32[5,64,256]{2,1,0:T(8,128)S(1)} fusion(f32[5,16,256]{2,1,0:T(8,128)S(1)} %fusion.53, f32[64,16,256]{2,1,0:T(8,128)S(1)} %get-tuple-element.51), kind=kLoop, calls=%fused_computation.5 | loop fusion | flops 2539520 | bytes 1458176 | tf_op jit(solution)/shard_map/while/body/eval_jaxpr/jvp()/reduce_sum | solution.py:79
  78.5 0.2 multiply_reduce_fusion.8
  78.7 0.2 fusion.14
  79.0 0.8 multiply_reduce_fusion.1
  79.8 0.5 multiply_reduce_fusion.4
  80.5 0.6 fusion.10
  81.0 0.8 fusion.9
  81.9 0.7 copy.65
  82.5 0.5 copy-done.2
  83.1 0.8 fusion.15
  83.9 2.0 %copy.54 = f32[3,16,256]{0,2,1:T(8,128)} copy(f32[3,16,256]{2,1,0:T(8,128)S(1)} %get-tuple-element.60) | data formatting | bytes 98304 | tf_op jit(solution)/shard_map/neg | solution.py:186
  85.9 23.4 %scatter_custom_fusion = f32[3,4608]{0,1:T(8,128)S(1)} fusion(s32[4096]{0:T(1024)} %bitcast.126, f32[4096,3]{1,0:T(8,128)} %bitcast.115, f32[]{:T(128)} %constant.144.clone.1), kind=kCustom, calls=%fused_computation.28 | custom fusion | flops 12288 | bytes 55808 | tf_op jit(solution)/shard_map/scatter-add | solution.py:186
  109.4 1.4 %fusion.118 = (f32[3,1,3,4,128]{0,4,3,2,1:T(8,128)}, f32[3,1,3,4,128]{0,4,3,2,1:T(8,128)S(1)}, f32[3,1,3,4,128]{0,4,3,2,1:T(8,128)}) fusion(f32[3,3,3,4,128]{0,4,3,2,1:T(8,128)S(1)} %bitcast.107), kind=kLoop, calls=%fused_computation.236 | loop fusion | bytes 110592 | tf_op jit(solution)/shard_map/slice | solution.py:96
  110.7 1.4 %copy.57 = f32[3,1,3,4,128]{4,3,2,1,0:T(4,128)S(1)} copy(f32[3,1,3,4,128]{0,4,3,2,1:T(8,128)} %get-tuple-element.52) | data formatting | bytes 36864
  112.2 1.4 %copy.58 = f32[3,1,3,4,128]{4,3,2,1,0:T(4,128)S(1)} copy(f32[3,1,3,4,128]{0,4,3,2,1:T(8,128)} %get-tuple-element.54) | data formatting | bytes 36864
  113.6 2.8 %collective-permute-start.13 = (f32[3,1,3,4,128]{4,3,2,1,0:T(4,128)S(1)}, f32[3,1,3,4,128]{4,3,2,1,0:T(4,128)S(1)}, u32[]{:S(2)}, u32[]{:S(2)}) collective-permute-start(f32[3,1,3,4,128]{4,3,2,1,0:T(4,128)S(1)} %copy.58), channel_id=1, source_target_pairs={{0,24},{8,0},{16,8},{24,16},{1,25},{9,1},{17,9},{25,17},{2,26},{10... | collective-permute-start | bytes 55304 | tf_op jit(solution)/shard_map/ppermute | solution.py:28
  116.5 0.3 copy.56
  116.8 1.5 %collective-permute-done.13 = f32[3,1,3,4,128]{4,3,2,1,0:T(4,128)S(1)} collective-permute-done((f32[3,1,3,4,128]{4,3,2,1,0:T(4,128)S(1)}, f32[3,1,3,4,128]{4,3,2,1,0:T(4,128)S(1)}, u32[]{:S(2)}, u32[]{:S(2)}) %collective-permute-start.13) | collective-permute-done | bytes 18464 | tf_op jit(solution)/shard_map/ppermute | solution.py:28
  118.4 0.5 collective-permute-start.15
  118.9 0.7 collective-permute-done.14
  119.8 1.2 collective-permute-start.16
  120.9 3.0 %collective-permute-start.17 = (f32[3,1,1,1,128]{4,3,2,1,0:T(1,128)S(1)}, f32[3,1,1,1,128]{4,3,2,1,0:T(1,128)S(1)}, u32[]{:S(2)}, u32[]{:S(2)}) collective-permute-start(f32[3,1,1,1,128]{4,3,2,1,0:T(1,128)S(1)} %get-tuple-element.72), channel_id=1, source_target_pairs={{0,3},{1,0},{2,1},{3,2},{4,7},{5,4},{6,5},{7,6},{8,11},{9,8},{10,9... | collective-permute-start | bytes 4616 | tf_op jit(solution)/shard_map/ppermute | solution.py:28
  123.9 0.6 fusion.107
  124.8 0.6 collective-permute-done.16
  125.4 0.6 fusion.103
  (87 shorter events, 1.6 us)
Async XLA Ops:
  0.6 72.3 %copy-start = (bf16[64,192]{1,0:T(8,128)(2,1)S(1)}, bf16[64,192]{1,0:T(8,128)(2,1)}, u32[]{:S(2)}) copy-start(bf16[64,192]{1,0:T(8,128)(2,1)} %param.20) | copy-start | bytes 73732
  1.4 10.4 %copy-start.6 = (f32[2,128]{1,0:T(2,128)}, f32[2,128]{1,0:T(2,128)S(1)}, u32[]{:S(2)}) copy-start(f32[2,128]{1,0:T(2,128)S(1)} %fusion.104) | copy-start | bytes 3076
  2.2 9.7 %copy-start.3 = (f32[2,128]{1,0:T(2,128)}, f32[2,128]{1,0:T(2,128)S(1)}, u32[]{:S(2)}) copy-start(f32[2,128]{1,0:T(2,128)S(1)} %fusion.97) | copy-start | bytes 3076
  3.5 20.0 %collective-permute-start = (f32[3,1,1,2,128]{4,3,2,1,0:T(2,128)S(1)}, f32[3,1,1,2,128]{4,3,2,1,0:T(2,128)S(1)}, u32[]{:S(2)}, u32[]{:S(2)}) collective-permute-start(f32[3,1,1,2,128]{4,3,2,1,0:T(2,128)S(1)} %get-tuple-element.35), channel_id=1, source_target_pairs={{0,8},{8,16},{16,24},{24,0},{1,9},{9,17},{17,25},{25,1},{2,10},{10... | collective-permute-start | bytes 9224 | tf_op jit(solution)/shard_map/ppermute | solution.py:19
  6.5 17.1 %collective-permute-start.1 = (f32[3,1,1,2,128]{4,3,2,1,0:T(2,128)S(1)}, f32[3,1,1,2,128]{4,3,2,1,0:T(2,128)S(1)}, u32[]{:S(2)}, u32[]{:S(2)}) collective-permute-start(f32[3,1,1,2,128]{4,3,2,1,0:T(2,128)S(1)} %get-tuple-element.35), channel_id=1, source_target_pairs={{8,0},{16,8},{24,16},{0,24},{9,1},{17,9},{25,17},{1,25},{10,2},{18... | collective-permute-start | bytes 9224 | tf_op jit(solution)/shard_map/ppermute | solution.py:20
  7.4 9.8 %collective-permute-start.6 = (s32[1,1,2,128]{3,2,1,0:T(2,128)}, s32[1,1,2,128]{3,2,1,0:T(2,128)S(1)}, u32[]{:S(2)}, u32[]{:S(2)}) collective-permute-start(s32[1,1,2,128]{3,2,1,0:T(2,128)} %param.15), channel_id=1, source_target_pairs={{0,8},{8,16},{16,24},{24,0},{1,9},{9,17},{17,25},{25,1},{2,10},{10... | collective-permute-start | bytes 3080 | tf_op jit(solution)/shard_map/ppermute | solution.py:19
  8.5 9.4 %collective-permute-start.7 = (s32[1,1,2,128]{3,2,1,0:T(2,128)}, s32[1,1,2,128]{3,2,1,0:T(2,128)S(1)}, u32[]{:S(2)}, u32[]{:S(2)}) collective-permute-start(s32[1,1,2,128]{3,2,1,0:T(2,128)} %param.15), channel_id=1, source_target_pairs={{8,0},{16,8},{24,16},{0,24},{9,1},{17,9},{25,17},{1,25},{10,2},{18... | collective-permute-start | bytes 3080 | tf_op jit(solution)/shard_map/ppermute | solution.py:20
  17.9 1.2 collective-permute-start.8
  18.0 1.3 %collective-permute-start.9 = (s32[3,1,2,128]{3,2,1,0:T(2,128)S(1)}, s32[3,1,2,128]{3,2,1,0:T(2,128)S(1)}, u32[]{:S(2)}, u32[]{:S(2)}) collective-permute-start(s32[3,1,2,128]{3,2,1,0:T(2,128)S(1)} %constant_dynamic-update-slice_fusion), channel_id=1, source_target_pairs={{4,0},{0,4},{5,1},{1,5},{6,2},{2,6},{7,3},{3,7},{12,8},{8,12},{13,... | collective-permute-start | bytes 9224 | tf_op jit(solution)/shard_map/ppermute | solution.py:20
  19.3 5.8 %collective-permute-start.10 = (s32[3,3,1,128]{3,2,1,0:T(1,128)S(1)}, s32[3,3,1,128]{3,2,1,0:T(1,128)S(1)}, u32[]{:S(2)}, u32[]{:S(2)}) collective-permute-start(s32[3,3,1,128]{3,2,1,0:T(1,128)S(1)} %get-tuple-element.69), channel_id=1, source_target_pairs={{0,1},{1,2},{2,3},{3,0},{4,5},{5,6},{6,7},{7,4},{8,9},{9,10},{10,1... | collective-permute-start | bytes 13832 | tf_op jit(solution)/shard_map/ppermute | solution.py:19
  21.4 3.7 %collective-permute-start.11 = (s32[3,3,1,128]{3,2,1,0:T(1,128)S(1)}, s32[3,3,1,128]{3,2,1,0:T(1,128)S(1)}, u32[]{:S(2)}, u32[]{:S(2)}) collective-permute-start(s32[3,3,1,128]{3,2,1,0:T(1,128)S(1)} %get-tuple-element.70), channel_id=1, source_target_pairs={{1,0},{2,1},{3,2},{0,3},{5,4},{6,5},{7,6},{4,7},{9,8},{10,9},{11,1... | collective-permute-start | bytes 13832 | tf_op jit(solution)/shard_map/ppermute | solution.py:20
  23.5 24.7 %collective-permute-start.2 = (f32[3,3,1,2,128]{4,3,2,1,0:T(2,128)S(1)}, f32[3,3,1,2,128]{4,3,2,1,0:T(2,128)S(1)}, u32[]{:S(2)}, u32[]{:S(2)}) collective-permute-start(f32[3,3,1,2,128]{4,3,2,1,0:T(2,128)S(1)} %pad_maximum_fusion.2), channel_id=1, source_target_pairs={{0,4},{4,0},{1,5},{5,1},{2,6},{6,2},{3,7},{7,3},{8,12},{12,8},{9,1... | collective-permute-start | bytes 27656 | tf_op jit(solution)/shard_map/ppermute | solution.py:19
  23.7 24.5 %collective-permute-start.3 = (f32[3,3,1,2,128]{4,3,2,1,0:T(2,128)S(1)}, f32[3,3,1,2,128]{4,3,2,1,0:T(2,128)S(1)}, u32[]{:S(2)}, u32[]{:S(2)}) collective-permute-start(f32[3,3,1,2,128]{4,3,2,1,0:T(2,128)S(1)} %pad_maximum_fusion.2), channel_id=1, source_target_pairs={{4,0},{0,4},{5,1},{1,5},{6,2},{2,6},{7,3},{3,7},{12,8},{8,12},{13,... | collective-permute-start | bytes 27656 | tf_op jit(solution)/shard_map/ppermute | solution.py:20
  25.1 27.3 %copy-start.5 = (bf16[10,64]{1,0:T(8,128)(2,1)S(1)}, bf16[10,64]{1,0:T(8,128)(2,1)}, u32[]{:S(2)}) copy-start(bf16[10,64]{1,0:T(8,128)(2,1)} %param.18) | copy-start | bytes 3844
  48.3 5.7 %collective-permute-start.4 = (f32[3,3,3,1,128]{4,3,2,1,0:T(1,128)S(1)}, f32[3,3,3,1,128]{4,3,2,1,0:T(1,128)S(1)}, u32[]{:S(2)}, u32[]{:S(2)}) collective-permute-start(f32[3,3,3,1,128]{4,3,2,1,0:T(1,128)S(1)} %get-tuple-element.62), channel_id=1, source_target_pairs={{0,1},{1,2},{2,3},{3,0},{4,5},{5,6},{6,7},{7,4},{8,9},{9,10},{10,1... | collective-permute-start | bytes 41480 | tf_op jit(solution)/shard_map/ppermute | solution.py:19
  49.8 4.1 %collective-permute-start.5 = (f32[3,3,3,1,128]{4,3,2,1,0:T(1,128)S(1)}, f32[3,3,3,1,128]{4,3,2,1,0:T(1,128)S(1)}, u32[]{:S(2)}, u32[]{:S(2)}) collective-permute-start(f32[3,3,3,1,128]{4,3,2,1,0:T(1,128)S(1)} %get-tuple-element.63), channel_id=1, source_target_pairs={{1,0},{2,1},{3,2},{0,3},{5,4},{6,5},{7,6},{4,7},{9,8},{10,9},{11,1... | collective-permute-start | bytes 41480 | tf_op jit(solution)/shard_map/ppermute | solution.py:20
  72.9 1.0 copy-start.1
  75.7 2.7 %copy-start.12 = (bf16[256,64]{0,1:T(8,128)(2,1)S(1)}, bf16[256,64]{0,1:T(8,128)(2,1)}, u32[]{:S(2)}) copy-start(bf16[256,64]{0,1:T(8,128)(2,1)} %param.21) | copy-start | bytes 98308
  75.7 2.7 %copy-start.13 = (f32[64]{0:T(128)S(1)}, f32[64]{0:T(128)}, u32[]{:S(2)}) copy-start(f32[64]{0:T(128)} %param.22) | copy-start | bytes 772
  75.7 2.7 %copy-start.14 = (bf16[64,256]{1,0:T(8,128)(2,1)S(1)}, bf16[64,256]{1,0:T(8,128)(2,1)}, u32[]{:S(2)}) copy-start(bf16[64,256]{1,0:T(8,128)(2,1)} %fusion.16) | copy-start | bytes 98308
  76.1 2.5 %copy-start.9 = (f32[256]{0:T(256)S(1)}, f32[256]{0:T(256)}, u32[]{:S(2)}) copy-start(f32[256]{0:T(256)} %fusion.105) | copy-start | bytes 3076
  81.8 1.2 copy-start.2
  81.8 1.2 copy-start.8
  81.9 1.2 copy-start.10
  109.3 14.6 %copy-start.11 = (s32[1,1,2]{2,1,0:T(1,128)S(1)}, s32[1,1,2]{2,1,0:T(1,128)}, u32[]{:S(2)}) copy-start(s32[1,1,2]{2,1,0:T(1,128)} %param.16) | copy-start | bytes 28
  109.3 16.1 %copy-start.4 = (f32[2,128]{1,0:T(2,128)S(1)}, f32[2,128]{1,0:T(2,128)}, u32[]{:S(2)}) copy-start(f32[2,128]{1,0:T(2,128)} %copy-done.3) | copy-start | bytes 3076
  109.4 16.1 %copy-start.7 = (f32[2,128]{1,0:T(2,128)S(1)}, f32[2,128]{1,0:T(2,128)}, u32[]{:S(2)}) copy-start(f32[2,128]{1,0:T(2,128)} %copy-done.6) | copy-start | bytes 3076
  112.1 4.7 %collective-permute-start.12 = (f32[3,1,3,4,128]{4,3,2,1,0:T(4,128)S(1)}, f32[3,1,3,4,128]{4,3,2,1,0:T(4,128)S(1)}, u32[]{:S(2)}, u32[]{:S(2)}) collective-permute-start(f32[3,1,3,4,128]{4,3,2,1,0:T(4,128)S(1)} %copy.57), channel_id=1, source_target_pairs={{0,8},{8,16},{16,24},{24,0},{1,9},{9,17},{17,25},{25,1},{2,10},{10... | collective-permute-start | bytes 55304 | tf_op jit(solution)/shard_map/ppermute | solution.py:28
  113.6 4.7 %collective-permute-start.13 = (f32[3,1,3,4,128]{4,3,2,1,0:T(4,128)S(1)}, f32[3,1,3,4,128]{4,3,2,1,0:T(4,128)S(1)}, u32[]{:S(2)}, u32[]{:S(2)}) collective-permute-start(f32[3,1,3,4,128]{4,3,2,1,0:T(4,128)S(1)} %copy.58), channel_id=1, source_target_pairs={{0,24},{8,0},{16,8},{24,16},{1,25},{9,1},{17,9},{25,17},{2,26},{10... | collective-permute-start | bytes 55304 | tf_op jit(solution)/shard_map/ppermute | solution.py:28
  118.4 1.2 collective-permute-start.14
  118.4 1.3 %collective-permute-start.15 = (f32[3,1,1,4,128]{4,3,2,1,0:T(4,128)S(1)}, f32[3,1,1,4,128]{4,3,2,1,0:T(4,128)S(1)}, u32[]{:S(2)}, u32[]{:S(2)}) collective-permute-start(f32[3,1,1,4,128]{4,3,2,1,0:T(4,128)S(1)} %get-tuple-element.65), channel_id=1, source_target_pairs={{0,4},{4,0},{1,5},{5,1},{2,6},{6,2},{3,7},{7,3},{8,12},{12,8},{9,1... | collective-permute-start | bytes 18440 | tf_op jit(solution)/shard_map/ppermute | solution.py:28
  119.8 5.7 %collective-permute-start.16 = (f32[3,1,1,1,128]{4,3,2,1,0:T(1,128)S(1)}, f32[3,1,1,1,128]{4,3,2,1,0:T(1,128)S(1)}, u32[]{:S(2)}, u32[]{:S(2)}) collective-permute-start(f32[3,1,1,1,128]{4,3,2,1,0:T(1,128)S(1)} %get-tuple-element.71), channel_id=1, source_target_pairs={{0,1},{1,2},{2,3},{3,0},{4,5},{5,6},{6,7},{7,4},{8,9},{9,10},{10,1... | collective-permute-start | bytes 4616 | tf_op jit(solution)/shard_map/ppermute | solution.py:28
  120.9 4.5 %collective-permute-start.17 = (f32[3,1,1,1,128]{4,3,2,1,0:T(1,128)S(1)}, f32[3,1,1,1,128]{4,3,2,1,0:T(1,128)S(1)}, u32[]{:S(2)}, u32[]{:S(2)}) collective-permute-start(f32[3,1,1,1,128]{4,3,2,1,0:T(1,128)S(1)} %get-tuple-element.72), channel_id=1, source_target_pairs={{0,3},{1,0},{2,1},{3,2},{4,7},{5,4},{6,5},{7,6},{8,11},{9,8},{10,9... | collective-permute-start | bytes 4616 | tf_op jit(solution)/shard_map/ppermute | solution.py:28
where the time goes:
time: 127 us; the launch traced here: 126 us
  local copies, waits for them, and re-layouts  52.9 us (42%)
  other arithmetic  38 us (30%)
  starting transfers between devices  24 us (19%)
  waiting for transfers between devices  5.18 us (4%)
  matrix products  4.71 us (4%)
    scatter-add x1, other arithmetic, shards(): sender_force.at[:, senders_all.reshape(-1)].add(-gradients.reshape(3, -1))  23.4 us
    gather x1, local copies, waits for them, and re-layouts, shards(): sender_kinds = ghost_kinds.reshape(-1)[senders_all]  23 us
    gather x2, local copies, waits for them, and re-layouts, shards(): ghost_pos_flat[:, senders_all]  16.4 us
    ppermute x6, starting transfers between devices, padded(): after = lax.ppermute(leading, axis, down)  8.41 us
    ppermute x6, starting transfers between devices, padded(): before = lax.ppermute(last, axis, up)  7.9 us
    ppermute x6, starting transfers between devices, shifted_2(): return lax.ppermute(value, axis, pairs)  7.7 us
    unnamed x46, local copies, waits for them, and re-layouts  7.06 us
    ppermute x6, waiting for transfers between devices, shifted_2(): return lax.ppermute(value, axis, pairs)  3.06 us
  transfers between devices with their start and end apart: 18, of which 9 were waited for; matrix products, arithmetic and copies ran while one was open for 27% of the time, Pallas kernels for 0%

commit v1 on v0

v1 whole, which is shorter than its diff:
```python
import functools
import itertools

import jax
import jax.numpy as jnp
from jax import lax
from jax.experimental import pallas as pl
from jax.experimental.pallas import tpu as pltpu
from jax.sharding import PartitionSpec as P

MASSES = (1.008, 12.011, 14.007, 15.999, 32.06, 22.99, 35.45, 39.098, 24.305, 40.078)
SQRT3 = 1.7320508075688772
HALF_SQRT3 = 0.8660254037844386
TIME_STEP = 0.5
AXES = ("gx", "gy", "gz")
MESH = pl.DeviceIdType.MESH
F32 = jnp.float32
BF16 = jnp.bfloat16
GROUP = 4


def canonical(coordinate, cells, total):
    return coordinate % total if total < cells + 2 else coordinate


def halo_plan(cells, sizes):
    totals = [c * s for c, s in zip(cells, sizes)]
    spans = [sorted({canonical(e, c, t) for e in range(-1, c + 1)}) for c, t in zip(cells, totals)]
    plan = []
    for at in itertools.product(*spans):
        step = tuple(e // c for e, c in zip(at, cells))
        inner = tuple(e % c for e, c in zip(at, cells))
        plan.append((at, step, inner))
    return spans, totals, plan


def dot(a, b, ca=1, cb=0):
    return lax.dot_general(a, b, (((ca,), (cb,)), ((), ())), preferred_element_type=F32)


def silu_parts(pre):
    sig = 0.5 * jnp.tanh(0.5 * pre) + 0.5
    return pre * sig, sig * (1.0 + pre * (1.0 - sig))


def harmonics(x, y, z):
    return (
        None,
        x,
        y,
        z,
        SQRT3 * x * y,
        SQRT3 * y * z,
        SQRT3 * z * x,
        HALF_SQRT3 * (x * x - y * y),
        0.5 * (2.0 * z * z - x * x - y * y),
    )


DEGREE = (0, 1, 1, 1, 2, 2, 2, 2, 2)


def step_kernel(
    sizes,
    frac,
    velocity,
    force_old,
    species,
    cell_count,
    neighbours,
    embed,
    w_in,
    w_out,
    w_node,
    w_energy,
    next_frac,
    next_velocity,
    next_force,
    site_energy,
    table,
    back,
    landed,
    onehot,
    spread,
    prod,
    feat_s,
    slope,
    basis_s,
    ysc,
    gsc,
    rows_s,
    msg,
    send_a,
    recv_a,
    send_b,
    recv_b,
):
    cells = species.shape[:3]
    cap = species.shape[3]
    cand = neighbours.shape[0]
    chan = embed.shape[1]
    kinds = embed.shape[0]
    nb = w_in.shape[0]
    spans, totals, plan = halo_plan(cells, sizes)
    index_of = {at: i for i, (at, _, _) in enumerate(plan)}
    inner_cells = list(itertools.product(*[range(c) for c in cells]))
    me = [lax.axis_index(a) for a in AXES]

    def device(step):
        return {
            a: lax.rem(m + s + n, n) for a, m, s, n in zip(AXES, me, step, sizes)
        }

    moves = [(i, step, inner) for i, (_, step, inner) in enumerate(plan) if any(s % n for s, n in zip(step, sizes))]
    others = sorted({tuple(s % n for s, n in zip(step, sizes)) for _, step, _ in moves})
    barrier = pltpu.get_barrier_semaphore()
    for step in others:
        pl.semaphore_signal(barrier, inc=1, device_id=device(step), device_id_type=MESH)

    rows = {}
    for c, (a, b, z) in enumerate(inner_cells):
        kind = species[a, b, pl.ds(z, 1), :]
        mass = jnp.zeros((1, cap), F32)
        for n, value in enumerate(MASSES):
            mass = jnp.where(kind == n, value / 16.0, mass)
        lane = lax.broadcasted_iota(jnp.int32, (1, cap), 1)
        occ = (lane < cell_count[a, b, z]).astype(F32)
        e = index_of[(a, b, z)]
        moved, half = [], []
        for d in range(3):
            h = velocity[d, a, b, pl.ds(z, 1), :] + 0.5 * TIME_STEP * force_old[d, a, b, pl.ds(z, 1), :] / mass
            m = frac[d, a, b, pl.ds(z, 1), :] + TIME_STEP * h
            table[e, d : d + 1, :] = m
            next_frac[d, a, b, pl.ds(z, 1), :] = occ * m
            half.append(h)
            moved.append(m)
        table[e, 3:4, :] = kind.astype(F32)
        rows[c] = (kind, mass, occ, moved, half)

    shift_bits = cap.bit_length() - 1
    pairs = {}
    slot_rows = lax.broadcasted_iota(jnp.int32, (cap, cap), 0)
    for c, (a, b, z) in enumerate(inner_cells):
        code = neighbours[:, a, b, z, :]
        if cap == 1 << shift_bits:
            offset, slot = code >> shift_bits, code & (cap - 1)
        else:
            offset, slot = code // cap, code % cap
        third = (offset * 43) >> 7
        ninth = (offset * 57) >> 9
        shifts = (ninth - 1, third - 3 * ninth - 1, offset - 3 * third - 1)
        cell = jnp.zeros_like(code)
        for axis in range(3):
            at = (a, b, z)[axis] + shifts[axis]
            low = spans[axis][0]
            if totals[axis] < cells[axis] + 2:
                at = jnp.where(at < 0, at + totals[axis], at)
                at = jnp.where(at >= totals[axis], at - totals[axis], at)
            cell = cell * len(spans[axis]) + (at - low)
        pairs[c] = (slot, cell, [s.astype(F32) for s in shifts])
        for k in range(cand):
            hit = slot_rows == slot[k : k + 1, :]
            onehot[:, pl.ds((c * cand + k) * cap, cap)] = jnp.where(hit, 1.0, 0.0).astype(BF16)

    pl.semaphore_wait(barrier, len(others))
    copies = []
    for i, step, inner in moves:
        copy = pltpu.make_async_remote_copy(
            src_ref=table.at[index_of[inner]],
            dst_ref=table.at[i],
            send_sem=send_a.at[i],
            recv_sem=recv_a.at[i],
            device_id=device(tuple(-s for s in step)),
            device_id_type=MESH,
        )
        copy.start()
        copies.append(copy)

    w_in_t = w_in[...].astype(F32).T.astype(BF16)
    w_out_t = w_out[...].astype(F32).T.astype(BF16)
    w_node_t = w_node[...].astype(F32).T.astype(BF16)
    diag = lax.broadcasted_iota(jnp.int32, (chan, chan), 0) == lax.broadcasted_iota(jnp.int32, (chan, chan), 1)
    energy_row = jnp.broadcast_to(w_energy[...], (chan, chan))
    energy_col = jnp.sum(jnp.where(diag, energy_row, 0.0), axis=1, keepdims=True)
    kind_rows = lax.broadcasted_iota(jnp.int32, (kinds, cap), 0)
    kind_rows_f = kind_rows.astype(F32)
    centres = lax.broadcasted_iota(jnp.int32, (nb, cap), 0).astype(F32) / (nb - 1)
    own_feat = {
        c: dot(embed[...], (kind_rows == rows[c][0]).astype(F32).astype(BF16), 0, 0).astype(BF16)
        for c in rows
    }

    for copy in copies:
        copy.wait_recv()

    geometry = {}
    for c, (a, b, z) in enumerate(inner_cells):
        slot, cell, shifts = pairs[c]
        found = [jnp.zeros((cand, cap), F32) for _ in range(4)]
        near = sorted(
            {
                index_of[tuple(canonical(p + s, n, t) for p, s, n, t in zip((a, b, z), move, cells, totals))]
                for move in itertools.product((-1, 0, 1), repeat=3)
            }
        )
        for e in near:
            hit = cell == e
            for q in range(4):
                row = jnp.broadcast_to(table[e, q : q + 1, :], (cand, cap))
                found[q] = jnp.where(hit, jnp.take_along_axis(row, slot, axis=1), found[q])
        x, y, w = [s + f - m for s, f, m in zip(shifts, found, rows[c][3])]
        squared = x * x + y * y + w * w
        rest = jnp.maximum(1.0 - squared, 0.0)
        envelope = rest * rest * rest
        geometry[c] = (x, y, w, squared, rest, envelope)
        at = pl.ds(c * cand, cand)
        rows_s[0, at, :] = squared
        rows_s[1, at, :] = found[3]
        for m, value in enumerate(harmonics(x, y, w)):
            ysc[m, at, :] = envelope if value is None else value * envelope

    groups = cand // GROUP
    for c, (a, b, z) in enumerate(inner_cells):
        occ = rows[c][2]
        msg[...] = jnp.zeros_like(msg)

        def forward(g, carry):
            first = c * cand + g * GROUP
            lanes = pl.ds(pl.multiple_of(first * cap, GROUP * cap), GROUP * cap)
            basis, hot = [], []
            for k in range(GROUP):
                gap = rows_s[0, pl.ds(first + k, 1), :] - centres
                basis.append(jnp.exp(-float((nb - 1) ** 2) * (gap * gap)))
                hot.append(jnp.where(kind_rows_f == rows_s[1, pl.ds(first + k, 1), :], 1.0, 0.0))
            basis = jnp.concatenate(basis, axis=1)
            hot = jnp.concatenate(hot, axis=1).astype(BF16)
            basis_s[:, lanes] = basis
            hidden, tilt = silu_parts(dot(w_in_t, basis.astype(BF16)))
            slope[:, lanes] = tilt
            radial = dot(w_out_t, hidden.astype(BF16))
            feat = dot(embed[...], hot, 0, 0)
            feat_s[:, lanes] = feat
            carried = [radial[d * chan : (d + 1) * chan] * feat for d in range(3)]
            for d in range(3):
                prod[d * chan : (d + 1) * chan, lanes] = carried[d]
            for m in range(9):
                total = msg[m]
                for k in range(GROUP):
                    weight = ysc[m, pl.ds(first + k, 1), :]
                    total = total + carried[DEGREE[m]][:, k * cap : (k + 1) * cap] * weight
                msg[m] = total
            return carry

        lax.fori_loop(0, groups, forward, 0)

        vector = msg[1] * msg[1] + msg[2] * msg[2] + msg[3] * msg[3]
        tensor = msg[4] * msg[4]
        for m in range(5, 9):
            tensor = tensor + msg[m] * msg[m]
        invariant = jnp.concatenate([msg[0].astype(BF16), vector.astype(BF16), tensor.astype(BF16), own_feat[c]], axis=0)
        active, tilt = silu_parts(dot(w_node_t, invariant))
        site_energy[a, b, pl.ds(z, 1), :] = occ * jnp.sum(energy_col * active, axis=0, keepdims=True)
        d_pre = (energy_col * occ * tilt).astype(BF16)
        d_inv = dot(w_node[0 : 3 * chan, :], d_pre).astype(BF16).astype(F32)
        msg[0] = d_inv[0:chan]
        for m in range(1, 9):
            part = d_inv[DEGREE[m] * chan : (DEGREE[m] + 1) * chan]
            msg[m] = 2.0 * msg[m] * part

        def backward(g, carry):
            first = c * cand + g * GROUP
            lanes = pl.ds(pl.multiple_of(first * cap, GROUP * cap), GROUP * cap)
            d_radial = []
            for k in range(GROUP):
                part = pl.ds(pl.multiple_of((first + k) * cap, cap), cap)
                sums = [None, None, None]
                for m in range(9):
                    d = DEGREE[m]
                    grad = msg[m]
                    gsc[m, pl.ds(first + k, 1), :] = jnp.sum(
                        prod[d * chan : (d + 1) * chan, part] * grad, axis=0, keepdims=True
                    )
                    term = grad * ysc[m, pl.ds(first + k, 1), :]
                    sums[d] = term if sums[d] is None else sums[d] + term
                feat = feat_s[:, part]
                d_radial.append(jnp.concatenate([(s * feat).astype(BF16) for s in sums], axis=0))
            d_radial = jnp.concatenate(d_radial, axis=1)
            d_hidden = dot(w_out[...], d_radial).astype(BF16).astype(F32)
            d_pre_h = (d_hidden * slope[:, lanes]).astype(BF16)
            d_basis = dot(w_in[...], d_pre_h).astype(BF16).astype(F32) * basis_s[:, lanes]
            for k in range(GROUP):
                gap = rows_s[0, pl.ds(first + k, 1), :] - centres
                piece = d_basis[:, k * cap : (k + 1) * cap] * gap
                rows_s[2, pl.ds(first + k, 1), :] = -2.0 * float((nb - 1) ** 2) * jnp.sum(
                    piece, axis=0, keepdims=True
                )
            return carry

        lax.fori_loop(0, groups, backward, 0)

    forces = {}
    quads = spread.shape[0] // 8
    sub = lax.broadcasted_iota(jnp.int32, (8, cap), 0)
    upper = (sub >= 4).astype(jnp.int32)
    for c, (a, b, z) in enumerate(inner_cells):
        x, y, w, squared, rest, envelope = geometry[c]
        at = pl.ds(c * cand, cand)
        grads = [gsc[m, at, :] for m in range(9)]
        d_env = grads[0]
        for m, value in enumerate(harmonics(x, y, w)):
            if m:
                d_env = d_env + value * grads[m]
        d_sq = 2.0 * (rows_s[2, at, :] - 3.0 * rest * rest * d_env)
        h = [None] + [envelope * grads[m] for m in range(1, 9)]
        gx = x * d_sq + h[1] + SQRT3 * (y * h[4] + w * h[6] + x * h[7]) - x * h[8]
        gy = y * d_sq + h[2] + SQRT3 * (x * h[4] + w * h[5] - y * h[7]) - y * h[8]
        gz = w * d_sq + h[3] + SQRT3 * (y * h[5] + x * h[6]) + 2.0 * w * h[8]
        gradient = (gx, gy, gz)
        forces[c] = [jnp.sum(g, axis=0, keepdims=True) for g in gradient]
        cell = pairs[c][1]
        for k in range(cand):
            block = jnp.zeros((8, cap), F32)
            for d in range(3):
                block = jnp.where((sub & 3) == d, -gradient[d][k : k + 1, :], block)
            where = cell[k : k + 1, :] - upper
            lanes = pl.ds((c * cand + k) * cap, cap)
            pieces = [jnp.where(where == 2 * q, block, 0.0) for q in range(quads)]
            spread[:, lanes] = jnp.concatenate(pieces, axis=0).astype(BF16)

    scattered = dot(spread[...], onehot[...], 1, 1)
    for i in range(len(plan)):
        back[i] = scattered[4 * i : 4 * i + 4]
    returns = []
    for i, step, inner in moves:
        copy = pltpu.make_async_remote_copy(
            src_ref=back.at[i],
            dst_ref=landed.at[i],
            send_sem=send_b.at[i],
            recv_sem=recv_b.at[i],
            device_id=device(step),
            device_id_type=MESH,
        )
        copy.start()
        returns.append(copy)
    for copy in copies:
        copy.wait_send()
    for copy in returns:
        copy.wait_recv()
    remote = {i for i, _, _ in moves}
    for c, (a, b, z) in enumerate(inner_cells):
        kind, mass, occ, moved, half = rows[c]
        total = jnp.zeros((4, cap), F32)
        for i, (_, _, inner) in enumerate(plan):
            if inner == (a, b, z):
                total = total + (landed[i] if i in remote else back[i])
        for d in range(3):
            force = occ * (forces[c][d] + total[d : d + 1])
            next_force[d, a, b, pl.ds(z, 1), :] = force
            next_velocity[d, a, b, pl.ds(z, 1), :] = occ * (half[d] + 0.5 * TIME_STEP * force / mass)
    for copy in returns:
        copy.wait_send()


def solution(mesh):
    sizes = tuple(mesh.shape[a] for a in AXES)

    def shards(frac, velocity, force_old, species, cell_count, neighbours, embed, w_in, w_out, w_node, w_energy):
        cells, cap = species.shape[:3], species.shape[3]
        cand, chan, nb = neighbours.shape[0], embed.shape[1], w_in.shape[0]
        _, _, plan = halo_plan(cells, sizes)
        count = cells[0] * cells[1] * cells[2]
        pair_rows = count * cand
        wide = pair_rows * cap
        held = len(plan)
        spread_rows = -(-4 * held // 16) * 16
        vmem = pl.BlockSpec(memory_space=pltpu.VMEM)
        smem = pl.BlockSpec(memory_space=pltpu.SMEM)
        field = jax.ShapeDtypeStruct(frac.shape, F32)
        return pl.pallas_call(
            functools.partial(step_kernel, sizes),
            out_shape=(field, field, field, jax.ShapeDtypeStruct(species.shape, F32)),
            in_specs=[vmem] * 4 + [smem] + [vmem] * 6,
            out_specs=(vmem,) * 4,
            scratch_shapes=[
                pltpu.VMEM((held, 4, cap), F32),
                pltpu.VMEM((held, 4, cap), F32),
                pltpu.VMEM((held, 4, cap), F32),
                pltpu.VMEM((cap, wide), BF16),
                pltpu.VMEM((spread_rows, wide), BF16),
                pltpu.VMEM((3 * chan, wide), F32),
                pltpu.VMEM((chan, wide), F32),
                pltpu.VMEM((chan, wide), F32),
                pltpu.VMEM((nb, wide), F32),
                pltpu.VMEM((9, pair_rows, cap), F32),
                pltpu.VMEM((9, pair_rows, cap), F32),
                pltpu.VMEM((3, pair_rows, cap), F32),
                pltpu.VMEM((9, chan, cap), F32),
                pltpu.SemaphoreType.DMA((held,)),
                pltpu.SemaphoreType.DMA((held,)),
                pltpu.SemaphoreType.DMA((held,)),
                pltpu.SemaphoreType.DMA((held,)),
            ],
            compiler_params=pltpu.CompilerParams(collective_id=0, has_side_effects=True),
        )(frac, velocity, force_old, species, cell_count, neighbours, embed, w_in, w_out, w_node, w_energy.reshape(1, -1))

    field = P(None, "gx", "gy", "gz", None)
    cell = P("gx", "gy", "gz", None)
    return jax.shard_map(
        shards,
        mesh=mesh,
        in_specs=(field, field, field, cell, P("gx", "gy", "gz"), field, P(), P(), P(), P(), P()),
        out_specs=(field, field, field, cell),
        check_vma=False,
    )
```

time: 127 us -> 33.8 us (0.27)
  local copies, waits for them, and re-layouts: 52.9 us -> 4.72 us
  other arithmetic: 38 us -> 0 us
  Pallas kernels: 0 us -> 28.1 us
  starting transfers between devices: 24 us -> 0 us
  waiting for transfers between devices: 5.18 us -> 0 us
  matrix products: 4.71 us -> 0 us
    gather x3 -> x0, local copies, waits for them, and re-layouts: 39.4 us -> none  [the longest x1 23 us: shards(): sender_kinds = ghost_kinds.reshape(-1)[senders_all]]
    pallas_call x0 -> x1, Pallas kernels: none -> 28.1 us  [shards(): pl.pallas_call(functools.partial(step_kernel, sizes), out_shape=(field, f...]
    ppermute x18 -> x0, starting transfers between devices: 24 us -> none  [the longest x6 8.41 us: padded(): after = lax.ppermute(leading, axis, down)]
    scatter-add x1 -> x0, other arithmetic: 23.4 us -> none  [shards(): sender_force.at[:, senders_all.reshape(-1)].add(-gradients.reshape(3, -1))]
    reduce_sum x10 -> x0, other arithmetic: 6.2 us -> none  [the longest x2 2.17 us: site_terms(): tensor_part = jnp.sum(carried[2][None] * second_order[:, None], axis=2)]
    ppermute x18 -> x0, waiting for transfers between devices: 5.18 us -> none  [the longest x6 3.06 us: shifted_2(): return lax.ppermute(value, axis, pairs)]
    dot_general x7 -> x0, matrix products: 4.71 us -> none  [the longest x2 1.86 us: embed_species(): jnp.dot(embed.T, onehot, preferred_element_type=jnp.float32)]
    mul x5 -> x0, other arithmetic: 3.72 us -> none  [the longest x1 1.31 us: shards(): next_frac = occupied * moved]
  transfers between devices with their start and end apart: 18 -> 0, of which waited for: 9 -> 0; matrix products, arithmetic and copies ran while one was open for 27% -> 0% of each run, Pallas kernels for 0% -> 0%
where the time goes in v1:
time: 33.8 us; the launch traced here: 33.5 us
  Pallas kernels  28.1 us (83%)
  local copies, waits for them, and re-layouts  4.72 us (14%)
  between operations  0.65 us (2%)
    pallas_call x1, Pallas kernels, shards(): pl.pallas_call(functools.partial(step_kernel, sizes), out_shape=(field, f...  28.1 us
    unnamed x13, local copies, waits for them, and re-layouts  4.72 us

profile of v1, /device:TPU:0, one launch (start us, length us, event | category | flops | bytes accessed | tf_op | source)
XLA Modules:
  0.0 33.5 jit_solution(11861387567691832905)
XLA Ops:
  0.6 1.5 %copy.15.w_node = bf16[256,64]{1,0:T(8,128)(2,1)} copy(bf16[256,64]{0,1:T(8,128)(2,1)} %param.20) | data formatting | bytes 65536 | tf_op args[9]
  2.1 28.1 %shard_map.138 = (f32[3,1,1,2,128]{4,3,2,1,0:T(2,128)}, f32[3,1,1,2,128]{4,3,2,1,0:T(2,128)}, f32[3,1,1,2,128]{4,3,2,1,0:T(2,128)}, f32[1,1,2,128]{3,2,1,0:T(2,128)}) custom-call(f32[3,1,1,2,128]{4,3,2,1,0:T(2,128)} %frac.1, f32[3,1,1,2,128]{4,3,2,1,0:T(2,128)} %velocity.1, f32[3,1,1,2,128]{4,3,2,1,0:T(2,128)} %force_old.1, s32[1,1,2,128]{3,2,1,0:T(2,128)} %species.1, ...), custom_call_target="tpu_custom_call" | custom-call | tf_op jit(solution)/shard_map/pallas_call | solution.py:379
  30.2 0.0 copy-start.2
  30.2 0.7 %copy-done.2 = f32[3,1,1,2,128]{4,3,2,1,0:T(2,128)S(1)} copy-done((f32[3,1,1,2,128]{4,3,2,1,0:T(2,128)S(1)}, f32[3,1,1,2,128]{4,3,2,1,0:T(2,128)}, u32[]{:S(2)}) %copy-start.2) | copy-done | bytes 3096
  30.9 0.0 copy-start.1
  30.9 0.6 %copy.20 = f32[3,1,1,2,128]{4,3,2,1,0:T(2,128)} copy(f32[3,1,1,2,128]{4,3,2,1,0:T(2,128)S(1)} %copy-done.2) | data formatting | bytes 6144
  31.5 0.1 copy-done.1
  31.6 0.0 copy-start
  31.6 0.6 %copy.21 = f32[3,1,1,2,128]{4,3,2,1,0:T(2,128)} copy(f32[3,1,1,2,128]{4,3,2,1,0:T(2,128)S(1)} %copy-done.1) | data formatting | bytes 6144
  32.2 0.1 copy-done
  32.3 0.0 copy-start.3
  32.3 0.6 %copy.22 = f32[3,1,1,2,128]{4,3,2,1,0:T(2,128)} copy(f32[3,1,1,2,128]{4,3,2,1,0:T(2,128)S(1)} %copy-done) | data formatting | bytes 6144
  32.8 0.1 copy-done.3
  32.9 0.6 %copy.23 = f32[1,1,2,128]{3,2,1,0:T(2,128)} copy(f32[1,1,2,128]{3,2,1,0:T(2,128)S(1)} %copy-done.3) | data formatting | bytes 2048
Async XLA Ops:
  30.2 0.7 %copy-start.2 = (f32[3,1,1,2,128]{4,3,2,1,0:T(2,128)S(1)}, f32[3,1,1,2,128]{4,3,2,1,0:T(2,128)}, u32[]{:S(2)}) copy-start(f32[3,1,1,2,128]{4,3,2,1,0:T(2,128)} %get-tuple-element.8) | copy-start | bytes 9220
  30.9 0.7 %copy-start.1 = (f32[3,1,1,2,128]{4,3,2,1,0:T(2,128)S(1)}, f32[3,1,1,2,128]{4,3,2,1,0:T(2,128)}, u32[]{:S(2)}) copy-start(f32[3,1,1,2,128]{4,3,2,1,0:T(2,128)} %get-tuple-element.9) | copy-start | bytes 9220
  31.6 0.7 %copy-start = (f32[3,1,1,2,128]{4,3,2,1,0:T(2,128)S(1)}, f32[3,1,1,2,128]{4,3,2,1,0:T(2,128)}, u32[]{:S(2)}) copy-start(f32[3,1,1,2,128]{4,3,2,1,0:T(2,128)} %get-tuple-element.10) | copy-start | bytes 9220
  32.3 0.7 %copy-start.3 = (f32[1,1,2,128]{3,2,1,0:T(2,128)S(1)}, f32[1,1,2,128]{3,2,1,0:T(2,128)}, u32[]{:S(2)}) copy-start(f32[1,1,2,128]{3,2,1,0:T(2,128)} %get-tuple-element.11) | copy-start | bytes 3076

commit v2 on v1

--- a/solution.py
+++ b/solution.py
@@ -16,7 +16,8 @@
 MESH = pl.DeviceIdType.MESH
 F32 = jnp.float32
 BF16 = jnp.bfloat16
-GROUP = 4
+GROUP = 16
+INPUTS = 11
 
 
 def canonical(coordinate, cells, total):
@@ -60,41 +61,16 @@
 DEGREE = (0, 1, 1, 1, 2, 2, 2, 2, 2)
 
 
-def step_kernel(
-    sizes,
-    frac,
-    velocity,
-    force_old,
-    species,
-    cell_count,
-    neighbours,
-    embed,
-    w_in,
-    w_out,
-    w_node,
-    w_energy,
-    next_frac,
-    next_velocity,
-    next_force,
-    site_energy,
-    table,
-    back,
-    landed,
-    onehot,
-    spread,
-    prod,
-    feat_s,
-    slope,
-    basis_s,
-    ysc,
-    gsc,
-    rows_s,
-    msg,
-    send_a,
-    recv_a,
-    send_b,
-    recv_b,
-):
+def step_kernel(sizes, *refs):
+    sources, outs, held = refs[:INPUTS], refs[INPUTS : INPUTS + 4], refs[INPUTS + 4 :]
+    next_frac, next_velocity, next_force, site_energy = outs
+    staged, held = held[:INPUTS], held[INPUTS:]
+    frac, velocity, force_old, species, cell_count, neighbours, embed, w_in, w_out, w_node_t, w_energy = staged
+    (table, back, landed, onehot, spread, prod, feat_s, slope, basis_s, ysc, gsc, rows_s, msg) = held[:13]
+    send_a, recv_a, send_b, recv_b, load_sem = held[13:]
+    loads = [pltpu.make_async_copy(sources[i], staged[i], load_sem.at[i]) for i in range(INPUTS)]
+    for load in loads:
+        load.start()
     cells = species.shape[:3]
     cap = species.shape[3]
     cand = neighbours.shape[0]
@@ -116,6 +92,9 @@
     barrier = pltpu.get_barrier_semaphore()
     for step in others:
         pl.semaphore_signal(barrier, inc=1, device_id=device(step), device_id_type=MESH)
+
+    for load in loads[:6]:
+        load.wait()
 
     rows = {}
     for c, (a, b, z) in enumerate(inner_cells):
@@ -176,9 +155,10 @@
         copy.start()
         copies.append(copy)
 
+    for load in loads[6:]:
+        load.wait()
     w_in_t = w_in[...].astype(F32).T.astype(BF16)
     w_out_t = w_out[...].astype(F32).T.astype(BF16)
-    w_node_t = w_node[...].astype(F32).T.astype(BF16)
     diag = lax.broadcasted_iota(jnp.int32, (chan, chan), 0) == lax.broadcasted_iota(jnp.int32, (chan, chan), 1)
     energy_row = jnp.broadcast_to(w_energy[...], (chan, chan))
     energy_col = jnp.sum(jnp.where(diag, energy_row, 0.0), axis=1, keepdims=True)
@@ -258,10 +238,10 @@
         for m in range(5, 9):
             tensor = tensor + msg[m] * msg[m]
         invariant = jnp.concatenate([msg[0].astype(BF16), vector.astype(BF16), tensor.astype(BF16), own_feat[c]], axis=0)
-        active, tilt = silu_parts(dot(w_node_t, invariant))
+        active, tilt = silu_parts(dot(w_node_t[...], invariant))
         site_energy[a, b, pl.ds(z, 1), :] = occ * jnp.sum(energy_col * active, axis=0, keepdims=True)
         d_pre = (energy_col * occ * tilt).astype(BF16)
-        d_inv = dot(w_node[0 : 3 * chan, :], d_pre).astype(BF16).astype(F32)
+        d_inv = dot(w_node_t[:, 0 : 3 * chan], d_pre, 0, 0).astype(BF16).astype(F32)
         msg[0] = d_inv[0:chan]
         for m in range(1, 9):
             part = d_inv[DEGREE[m] * chan : (DEGREE[m] + 1) * chan]
@@ -361,6 +341,12 @@
         copy.wait_send()
 
 
+def hand_over(*refs):
+    half = len(refs) // 2
+    for source, target in zip(refs[:half], refs[half:]):
+        target[...] = source[...]
+
+
 def solution(mesh):
     sizes = tuple(mesh.shape[a] for a in AXES)
 
@@ -374,14 +360,19 @@
         held = len(plan)
         spread_rows = -(-4 * held // 16) * 16
         vmem = pl.BlockSpec(memory_space=pltpu.VMEM)
-        smem = pl.BlockSpec(memory_space=pltpu.SMEM)
+        operands = (frac, velocity, force_old, species, cell_count, neighbours)
+        operands += (embed, w_in, w_out, w_node.T, w_energy.reshape(1, -1))
+        staged = [pltpu.VMEM(o.shape, o.dtype) for o in operands]
+        staged[4] = pltpu.SMEM(cell_count.shape, cell_count.dtype)
         field = jax.ShapeDtypeStruct(frac.shape, F32)
-        return pl.pallas_call(
+        results = (field, field, field, jax.ShapeDtypeStruct(species.shape, F32))
+        outs = pl.pallas_call(
             functools.partial(step_kernel, sizes),
-            out_shape=(field, field, field, jax.ShapeDtypeStruct(species.shape, F32)),
-            in_specs=[vmem] * 4 + [smem] + [vmem] * 6,
+            out_shape=results,
+            in_specs=[pl.BlockSpec(memory_space=pl.ANY)] * INPUTS,
             out_specs=(vmem,) * 4,
-            scratch_shapes=[
+            scratch_shapes=staged
+            + [
                 pltpu.VMEM((held, 4, cap), F32),
                 pltpu.VMEM((held, 4, cap), F32),
                 pltpu.VMEM((held, 4, cap), F32),
@@ -399,9 +390,11 @@
                 pltpu.SemaphoreType.DMA((held,)),
                 pltpu.SemaphoreType.DMA((held,)),
                 pltpu.SemaphoreType.DMA((held,)),
+                pltpu.SemaphoreType.DMA((INPUTS,)),
             ],
             compiler_params=pltpu.CompilerParams(collective_id=0, has_side_effects=True),
-        )(frac, velocity, force_old, species, cell_count, neighbours, embed, w_in, w_out, w_node, w_energy.reshape(1, -1))
+        )(*operands)
+        return pl.pallas_call(hand_over, out_shape=results, in_specs=[vmem] * 4, out_specs=(vmem,) * 4)(*outs)
 
     field = P(None, "gx", "gy", "gz", None)
     cell = P("gx", "gy", "gz", None)

time: 33.8 us -> 25.8 us (0.76)
  local copies, waits for them, and re-layouts: 4.72 us -> 0 us
  Pallas kernels: 28.1 us -> 25 us
    unnamed x13 -> x0, local copies, waits for them, and re-layouts: 4.72 us -> none
    pallas_call x1 -> x2, Pallas kernels: 28.1 us -> 25 us  [the longest x1 23.7 us: shards(): pl.pallas_call(functools.partial(step_kernel, sizes), out_shape=results,...]
where the time goes in v2:
time: 25.8 us; the launch traced here: 25.6 us
  Pallas kernels  25 us (97%)
  between operations  0.64 us (2%)
    pallas_call x1, Pallas kernels, shards(): pl.pallas_call(functools.partial(step_kernel, sizes), out_shape=results,...  23.7 us
    pallas_call x1, Pallas kernels, shards(): pl.pallas_call(hand_over, out_shape=results, in_specs=[vmem] * 4, out_spe...  1.3 us

profile of v2, /device:TPU:0, one launch (start us, length us, event | category | flops | bytes accessed | tf_op | source)
XLA Modules:
  0.0 25.6 jit_solution(2831936850781771224)
XLA Ops:
  0.6 23.7 %shard_map.138 = (f32[3,1,1,2,128]{4,3,2,1,0:T(2,128)}, f32[3,1,1,2,128]{4,3,2,1,0:T(2,128)}, f32[3,1,1,2,128]{4,3,2,1,0:T(2,128)}, f32[1,1,2,128]{3,2,1,0:T(2,128)}) custom-call(f32[3,1,1,2,128]{4,3,2,1,0:T(2,128)} %refs_0_.1, f32[3,1,1,2,128]{4,3,2,1,0:T(2,128)} %refs_1_.1, f32[3,1,1,2,128]{4,3,2,1,0:T(2,128)} %refs_2_.1, s32[1,1,2,128]{3,2,1,0:T(2,128)} %refs_3_.1, ...), custom_call_target="tpu_custom_call" | custom-call | tf_op jit(solution)/shard_map/pallas_call | solution.py:369
  24.3 1.3 %shard_map.139 = (f32[3,1,1,2,128]{4,3,2,1,0:T(2,128)}, f32[3,1,1,2,128]{4,3,2,1,0:T(2,128)}, f32[3,1,1,2,128]{4,3,2,1,0:T(2,128)}, f32[1,1,2,128]{3,2,1,0:T(2,128)}) custom-call(f32[3,1,1,2,128]{4,3,2,1,0:T(2,128)} %get-tuple-element.8.refs_0_, f32[3,1,1,2,128]{4,3,2,1,0:T(2,128)} %get-tuple-element.9.refs_1_, ...), custom_call_target="tpu_custom_call" | custom-call | tf_op jit(solution)/shard_map/pallas_call | solution.py:397

commit v3 on v2

--- a/solution.py
+++ b/solution.py
@@ -37,6 +37,17 @@
 
 def dot(a, b, ca=1, cb=0):
     return lax.dot_general(a, b, (((ca,), (cb,)), ((), ())), preferred_element_type=F32)
+
+
+def repeat(count, body):
+    if count == 1:
+        body(0, 0)
+    else:
+        lax.fori_loop(0, count, body, 0)
+
+
+def aligned(start, unit):
+    return start if isinstance(start, int) else pl.multiple_of(start, unit)
 
 
 def silu_parts(pre):
@@ -68,6 +79,7 @@
     frac, velocity, force_old, species, cell_count, neighbours, embed, w_in, w_out, w_node_t, w_energy = staged
     (table, back, landed, onehot, spread, prod, feat_s, slope, basis_s, ysc, gsc, rows_s, msg) = held[:13]
     send_a, recv_a, send_b, recv_b, load_sem = held[13:]
+    sums_of = msg
     loads = [pltpu.make_async_copy(sources[i], staged[i], load_sem.at[i]) for i in range(INPUTS)]
     for load in loads:
         load.start()
@@ -201,12 +213,12 @@
 
     groups = cand // GROUP
     for c, (a, b, z) in enumerate(inner_cells):
-        occ = rows[c][2]
-        msg[...] = jnp.zeros_like(msg)
-
-        def forward(g, carry):
+        msg = sums_of.at[c]
+        msg[...] = jnp.zeros((9, chan, cap), F32)
+
+        def forward(g, carry, c=c, msg=msg):
             first = c * cand + g * GROUP
-            lanes = pl.ds(pl.multiple_of(first * cap, GROUP * cap), GROUP * cap)
+            lanes = pl.ds(aligned(first * cap, GROUP * cap), GROUP * cap)
             basis, hot = [], []
             for k in range(GROUP):
                 gap = rows_s[0, pl.ds(first + k, 1), :] - centres
@@ -231,8 +243,10 @@
                 msg[m] = total
             return carry
 
-        lax.fori_loop(0, groups, forward, 0)
-
+        repeat(groups, forward)
+
+    for c, (a, b, z) in enumerate(inner_cells):
+        occ, msg = rows[c][2], sums_of.at[c]
         vector = msg[1] * msg[1] + msg[2] * msg[2] + msg[3] * msg[3]
         tensor = msg[4] * msg[4]
         for m in range(5, 9):
@@ -247,12 +261,15 @@
             part = d_inv[DEGREE[m] * chan : (DEGREE[m] + 1) * chan]
             msg[m] = 2.0 * msg[m] * part
 
-        def backward(g, carry):
+    for c, (a, b, z) in enumerate(inner_cells):
+        msg = sums_of.at[c]
+
+        def backward(g, carry, c=c, msg=msg):
             first = c * cand + g * GROUP
-            lanes = pl.ds(pl.multiple_of(first * cap, GROUP * cap), GROUP * cap)
+            lanes = pl.ds(aligned(first * cap, GROUP * cap), GROUP * cap)
             d_radial = []
             for k in range(GROUP):
-                part = pl.ds(pl.multiple_of((first + k) * cap, cap), cap)
+                part = pl.ds(aligned((first + k) * cap, cap), cap)
                 sums = [None, None, None]
                 for m in range(9):
                     d = DEGREE[m]
@@ -276,7 +293,7 @@
                 )
             return carry
 
-        lax.fori_loop(0, groups, backward, 0)
+        repeat(groups, backward)
 
     forces = {}
     quads = spread.shape[0] // 8
@@ -385,7 +402,7 @@
                 pltpu.VMEM((9, pair_rows, cap), F32),
                 pltpu.VMEM((9, pair_rows, cap), F32),
                 pltpu.VMEM((3, pair_rows, cap), F32),
-                pltpu.VMEM((9, chan, cap), F32),
+                pltpu.VMEM((count, 9, chan, cap), F32),
                 pltpu.SemaphoreType.DMA((held,)),
                 pltpu.SemaphoreType.DMA((held,)),
                 pltpu.SemaphoreType.DMA((held,)),

time: 25.8 us -> 25.3 us (0.981)
  Pallas kernels: 25 us -> 24.4 us
    pallas_call x1, Pallas kernels: 23.7 us -> 23.2 us  [shards(): pl.pallas_call(functools.partial(step_kernel, sizes), out_shape=results,...]
where the time goes in v3:
time: 25.3 us; the launch traced here: 25.1 us
  Pallas kernels  24.4 us (96%)
  between operations  0.64 us (3%)
    pallas_call x1, Pallas kernels, shards(): pl.pallas_call(functools.partial(step_kernel, sizes), out_shape=results,...  23.2 us
    pallas_call x1, Pallas kernels, shards(): pl.pallas_call(hand_over, out_shape=results, in_specs=[vmem] * 4, out_spe...  1.3 us

profile of v3, /device:TPU:0, one launch (start us, length us, event | category | flops | bytes accessed | tf_op | source)
XLA Modules:
  0.0 25.1 jit_solution(1003798376099991774)
XLA Ops:
  0.6 23.2 %shard_map.138 = (f32[3,1,1,2,128]{4,3,2,1,0:T(2,128)}, f32[3,1,1,2,128]{4,3,2,1,0:T(2,128)}, f32[3,1,1,2,128]{4,3,2,1,0:T(2,128)}, f32[1,1,2,128]{3,2,1,0:T(2,128)}) custom-call(f32[3,1,1,2,128]{4,3,2,1,0:T(2,128)} %refs_0_.1, f32[3,1,1,2,128]{4,3,2,1,0:T(2,128)} %refs_1_.1, f32[3,1,1,2,128]{4,3,2,1,0:T(2,128)} %refs_2_.1, s32[1,1,2,128]{3,2,1,0:T(2,128)} %refs_3_.1, ...), custom_call_target="tpu_custom_call" | custom-call | tf_op jit(solution)/shard_map/pallas_call | solution.py:386
  23.8 1.3 %shard_map.139 = (f32[3,1,1,2,128]{4,3,2,1,0:T(2,128)}, f32[3,1,1,2,128]{4,3,2,1,0:T(2,128)}, f32[3,1,1,2,128]{4,3,2,1,0:T(2,128)}, f32[1,1,2,128]{3,2,1,0:T(2,128)}) custom-call(f32[3,1,1,2,128]{4,3,2,1,0:T(2,128)} %get-tuple-element.8.refs_0_, f32[3,1,1,2,128]{4,3,2,1,0:T(2,128)} %get-tuple-element.9.refs_1_, ...), custom_call_target="tpu_custom_call" | custom-call | tf_op jit(solution)/shard_map/pallas_call | solution.py:414
